TPU v7x, 256 devices: a whole 4x4x8 slice. The times are simulated.
256 devices in a mesh: blk: 64 (over x, z, y_lo), uly: 4 (over y_hi, core).
Axes of the slice: x: 4, y: 4 (y_hi: 2, y_lo: 2; y = y_hi * 2 + y_lo), z: 8, core: 2. Of those that a mesh axis runs over, the one named last changes fastest.
Arguments:
- tokens: bfloat16 [6144, 2560], P(('blk', 'uly')), may hold values from -6 to 6
- in_bits: int32 [6144, 2560], P(('blk', 'uly')), may hold values from 0 to 1
- qkv_weights: bfloat16 [2, 3, 2560, 2560], P(None, None, 'blk', 'uly'), may hold values from -0.125 to 0.125
- qkv_bits: int32 [6144, 3, 2560], P('blk', None, 'uly'), may hold values from 0 to 1
- gain_query: float32 [2560], P('uly'), may hold values from 0.7 to 1.8
- gain_key: float32 [2560], P('uly'), may hold values from 0.7 to 1.8
- out_weights: bfloat16 [2, 2560, 2560], P(None, 'uly', 'blk'), may hold values from -0.5 to 0.5
- mix_bits: int32 [6144, 2560], P('blk', 'uly'), may hold values from 0 to 1
- out_bits: int32 [6144, 2560], P('blk'), may hold values from 0 to 1
Outputs:
- layer_output: bfloat16 [6144, 2560], P(('blk', 'uly'))
Inputs may be any that keep to these rules, and one draw needn't show every extreme that they name: `in_bits`: a bit of 1 stands for the sign +1, a bit of 0 for -1. `qkv_bits`: a bit of 1 stands for the sign +1, a bit of 0 for -1. `mix_bits`: a bit of 1 stands for the sign +1, a bit of 0 for -1. `out_bits`: a bit of 1 stands for the sign +1, a bit of 0 for -1.
All inputs are finite; a program needn't handle non-finite values.
Results may differ from a plain program's by a relative error of at most 0.018.
Values may be sent and summed in bfloat16 or wider, within the bound.
A program may use at most 128 MiB of HBM per device.

v0:
```python
import math
import jax
import jax.numpy as jnp
from jax import lax
from jax.sharding import PartitionSpec as P

HEAD = 128
epsilon = 1e-06


def signed(bit_values):
    return (2 * bit_values - 1).astype(jnp.float32)


def normalize(values, gain_vector):
    row_count = values.shape[0]
    by_head = values.astype(jnp.float32).reshape(row_count, -1, HEAD)
    inverse_rms = lax.rsqrt(jnp.mean(by_head * by_head, axis=-1, keepdims=True) + epsilon)
    return (by_head * inverse_rms * gain_vector.reshape(-1, HEAD)).astype(jnp.bfloat16)


def body(
    tokens, in_bits, qkv_weights, qkv_bits, gain_query, gain_key, out_weights, mix_bits, out_bits
):
    flipped = (tokens.astype(jnp.float32) * signed(in_bits)).astype(jnp.bfloat16)
    group_rows = lax.all_gather(jnp.stack([tokens, flipped]), "uly", axis=1, tiled=True)
    row_total = group_rows.shape[1]
    projections = jnp.einsum(
        "mrd,mkdc->rmkc",
        group_rows,
        lax.all_gather(qkv_weights, "blk", axis=2, tiled=True),
        preferred_element_type=jnp.float32,
    )
    projected = (projections[:, 0] + signed(qkv_bits) * projections[:, 1]).astype(jnp.bfloat16)
    queries = normalize(projected[:, 0], gain_query)
    head_count = queries.shape[1]
    keys_normed = normalize(projected[:, 1], gain_key).reshape(row_total, -1)
    values_block = projected[:, 2]
    score_scale = 1.0 / math.sqrt(HEAD)

    def attend(running, shard_piece):
        numerator, denominator = running
        key_rows = shard_piece[0].reshape(shard_piece[0].shape[0], head_count, HEAD)
        value_rows = shard_piece[1].reshape(shard_piece[1].shape[0], head_count, HEAD)
        scores = (
            jnp.einsum("rhd,nhd->hrn", queries, key_rows, preferred_element_type=jnp.float32)
            * score_scale
        )
        weights = jnp.exp(scores).astype(jnp.bfloat16)
        numerator = numerator + jnp.einsum(
            "hrn,nhd->rhd", weights, value_rows, preferred_element_type=jnp.float32
        )
        denominator = denominator + jnp.sum(weights.astype(jnp.float32), axis=2).T
        return (numerator, denominator)

    start_state = (
        jnp.zeros((row_total, head_count, HEAD), jnp.float32),
        jnp.zeros((row_total, head_count), jnp.float32),
    )
    all_keys, all_values = (
        lax.all_gather(keys_normed, "blk", axis=0, tiled=True),
        lax.all_gather(values_block, "blk", axis=0, tiled=True),
    )
    group_count = lax.axis_size("blk")
    per_block = 1
    while per_block * row_total < 512 and group_count % (per_block * 2) == 0:
        per_block = per_block * 2
    block_rows = per_block * row_total
    block_count = group_count // per_block
    key_blocks = all_keys.reshape(block_count, block_rows, all_keys.shape[1])
    value_blocks = all_values.reshape(block_count, block_rows, all_values.shape[1])

    def scan_step(running, block_pair):
        return (attend(running, block_pair), None)

    (numerator, denominator), unused = lax.scan(scan_step, start_state, (key_blocks, value_blocks))
    attended = (numerator / denominator[:, :, None]).astype(jnp.bfloat16).reshape(row_total, -1)
    attended_flipped = (attended.astype(jnp.float32) * signed(mix_bits)).astype(jnp.bfloat16)
    attended_pair = jnp.stack([attended, attended_flipped])
    out_signs = signed(out_bits)
    partial_out = jnp.einsum(
        "mrc,mcn->rmn",
        attended_pair,
        lax.all_gather(out_weights, "blk", axis=2, tiled=True),
        preferred_element_type=jnp.float32,
    )
    summed = lax.psum_scatter(
        partial_out.astype(jnp.bfloat16), "uly", scatter_dimension=0, tiled=True
    ).astype(jnp.float32)
    own_rows = summed.shape[0]
    own_signs = lax.dynamic_slice_in_dim(out_signs, lax.axis_index("uly") * own_rows, own_rows, 0)
    result_rows = summed[:, 0] + own_signs * summed[:, 1]
    return result_rows.astype(jnp.bfloat16)


def solution(mesh):
    return jax.shard_map(
        body,
        mesh=mesh,
        in_specs=(
            P(("blk", "uly"), None),
            P(("blk", "uly"), None),
            P(None, None, "blk", "uly"),
            P("blk", None, "uly"),
            P("uly"),
            P("uly"),
            P(None, "uly", "blk"),
            P("blk", "uly"),
            P("blk", None),
        ),
        out_specs=P(("blk", "uly"), None),
        check_vma=False,
    )
```

profile of v0, /device:TPU:1, one launch (start us, length us, event | category | flops | bytes accessed | tf_op | source)
XLA Modules:
  0.0 1435.4 jit_solution(2879353111804736999)
XLA Ops:
  6.5 0.7 all-gather.6.cloned.1.call-update
  7.3 1.1 fusion.17
  8.4 0.9 pad_maximum_fusion
  9.3 12.7 all_gather.15
  22.0 423.9 %all-gather.6.cloned.1.call-done = bf16[2,3,2560,640]{3,2,1,0:T(8,128)(2,1)} async-done(((bf16[2,3,40,640]{3,2,1,0:T(8,128)(2,1)}), bf16[2,3,2560,640]{3,2,1,0:T(8,128)(2,1)}) %all-gather.6.cloned.1.call-update) | async-done | bytes 19660816 | tf_op jit(solution)/shard_map/all_gather | solution.py:31
  445.9 8.3 convolution_bitcast_fusion.1
  454.2 0.2 fusion.5
  454.4 0.2 copy.28
  454.8 0.7 fusion.8
  455.6 0.7 slice_convert_fusion
  456.4 0.5 all-gather.10.cloned.1.call-update
  457.0 0.2 copy.30
  457.5 268.4 %all-gather.8.cloned.1.call-done = bf16[6144,640]{1,0:T(8,128)(2,1)} async-done(((bf16[96,640]{1,0:T(8,128)(2,1)}), bf16[6144,640]{1,0:T(8,128)(2,1)}) %all-gather.8.cloned.1.call-update) | async-done | bytes 7864336 | tf_op jit(solution)/shard_map/all_gather | solution.py:61
  726.0 311.0 %all-gather.12.cloned.1.call-done = bf16[6144,1,640]{2,0,1:T(8,128)(2,1)} async-done(((bf16[96,1,640]{2,0,1:T(8,128)(2,1)}), bf16[6144,1,640]{2,0,1:T(8,128)(2,1)}) %all-gather.12.cloned.1.call-update) | async-done | bytes 7864336 | tf_op jit(solution)/shard_map/all_gather | solution.py:62
  1037.0 31.7 %while.13 = (s32[]{:T(128)}, f32[96,5,128]{2,0,1:T(8,128)S(1)}, f32[96,5]{0,1:T(8,128)S(1)}, bf16[8,768,640]{2,1,0:T(8,128)(2,1)}, bf16[8,768,640]{2,1,0:T(8,128...) while((s32[]{:T(128)}, f32[96,5,128]{2,0,1:T(8,128)S(1)}, ...), condition=%wide.region_4.5_spmd.clone, body=%wide.region_2.4_spmd.clone.sunk | while | flops 190341600 | bytes 11927140 | solution.py:76
  1037.0 1.7 constant_dynamic-slice_fusion.3
  1038.7 0.6 copy.51
  1039.3 0.5 convert_reduce_fusion.2
  1039.8 0.6 copy.50
  1040.5 0.5 fusion.35
  1040.9 1.7 constant_dynamic-slice_fusion.3
  1042.6 0.6 copy.51
  1043.3 0.5 convert_reduce_fusion.2
  1043.8 0.6 copy.50
  1044.4 0.5 fusion.35
  1044.9 1.7 constant_dynamic-slice_fusion.3
  1046.6 0.6 copy.51
  1047.3 0.5 convert_reduce_fusion.2
  1047.7 0.6 copy.50
  1048.4 0.5 fusion.35
  1048.9 1.7 constant_dynamic-slice_fusion.3
  1050.6 0.6 copy.51
  1051.2 0.5 convert_reduce_fusion.2
  1051.7 0.6 copy.50
  1052.4 0.5 fusion.35
  1052.9 1.7 constant_dynamic-slice_fusion.3
  1054.5 0.6 copy.51
  1055.2 0.5 convert_reduce_fusion.2
  1055.7 0.6 copy.50
  1056.3 0.5 fusion.35
  1056.8 1.7 constant_dynamic-slice_fusion.3
  1058.5 0.6 copy.51
  1059.2 0.5 convert_reduce_fusion.2
  1059.6 0.6 copy.50
  1060.3 0.5 fusion.35
  1060.8 1.7 constant_dynamic-slice_fusion.3
  1062.5 0.6 copy.51
  1063.1 0.5 convert_reduce_fusion.2
  1063.6 0.6 copy.50
  1064.3 0.5 fusion.35
  1064.8 1.7 constant_dynamic-slice_fusion.3
  1066.4 0.6 copy.51
  1067.1 0.5 convert_reduce_fusion.2
  1067.6 0.6 copy.50
  1068.2 0.5 fusion.35
  1069.0 0.2 copy.34
  1069.2 0.2 copy.36
  1069.5 1.0 fusion.18
  1070.5 274.9 %all-gather.10.cloned.1.call-done = bf16[2,640,2560]{1,2,0:T(8,128)(2,1)} async-done(((bf16[2,640,40]{1,2,0:T(8,128)(2,1)}), bf16[2,640,2560]{1,2,0:T(8,128)(2,1)}) %all-gather.10.cloned.1.call-update) | async-done | bytes 6553616 | tf_op jit(solution)/shard_map/all_gather | solution.py:84
  1345.4 5.0 fusion.1
  1350.3 1.0 copy.46
  1351.4 74.8 %reduce-scatter.4.cloned.1.call-done = bf16[24,5120]{1,0:T(8,128)(2,1)} async-done(((bf16[96,5120]{1,0:T(8,128)(2,1)}), bf16[24,5120]{1,0:T(8,128)(2,1)}) %reduce-scatter.4.cloned.1.call-update) | async-done | bytes 245776
  1426.2 1.0 bitcast_convert_fusion
  1427.2 1.7 fusion.11
  (36 shorter events, 1.3 us)
Async XLA Ops:
  6.5 439.4 %all-gather.6.cloned.1.call-start = ((), (), s32[]{:S(2)}) async-start(), calls=%async_computation.1 | async-start | bytes 19968000 | tf_op jit(solution)/shard_map/all_gather | solution.py:31
  7.3 718.7 %all-gather.8.cloned.1.call-start = ((), (), s32[]{:S(2)}) async-start(), calls=%async_computation.2 | async-start | bytes 7987200 | tf_op jit(solution)/shard_map/all_gather | solution.py:61
  22.0 432.2 %copy-start = (s32[96,3,640]{2,0,1:T(8,128)S(1)}, s32[96,3,640]{2,0,1:T(8,128)}, u32[]{:S(2)}) copy-start(s32[96,3,640]{2,0,1:T(8,128)} %param.14) | copy-start | bytes 2211844
  22.0 432.8 %copy-start.1 = (f32[640]{0:T(1024)S(1)}, f32[640]{0:T(1024)}, u32[]{:S(2)}) copy-start(f32[640]{0:T(1024)} %param.16) | copy-start | bytes 7684
  454.2 3.0 copy-start.2
  455.6 581.4 %all-gather.12.cloned.1.call-start = ((), (), s32[]{:S(2)}) async-start(), calls=%async_computation.4 | async-start | bytes 7987200 | tf_op jit(solution)/shard_map/all_gather | solution.py:62
  456.3 889.0 %all-gather.10.cloned.1.call-start = ((), (), s32[]{:S(2)}) async-start(), calls=%async_computation.3 | async-start | bytes 6656000 | tf_op jit(solution)/shard_map/all_gather | solution.py:84
  456.9 969.3 %reduce-scatter.4.cloned.1.call-start = ((), (), s32[]{:S(2)}) async-start(), calls=%async_computation.5 | async-start | bytes 1228800
Sparse Core Ops, SparseCore 0:
  9.2 436.6 all-gather.5
  455.7 270.2 all-gather.7
  727.7 309.1 all-gather.11
  1038.6 306.6 all-gather.9
  1351.5 74.6 reduce-scatter.3
where the time goes:
time: 1440 us
  waiting for transfers between devices  1350 us (94%)
  local copies, waits for them, and re-layouts  26.1 us (2%)
  matrix products  20.8 us (1%)
    all_gather x1, waiting for transfers between devices, body(): lax.all_gather(qkv_weights, 'blk', axis=2, tiled=True)  424 us
    all_gather x1, waiting for transfers between devices, body(): lax.all_gather(values_block, 'blk', axis=0, tiled=True)  311 us
    all_gather x1, waiting for transfers between devices, body(): lax.all_gather(out_weights, 'blk', axis=2, tiled=True)  275 us
    all_gather x1, waiting for transfers between devices, body(): lax.all_gather(keys_normed, 'blk', axis=0, tiled=True)  268 us
    unnamed x6, waiting for transfers between devices  76.1 us
  transfers between devices with their start and end apart: 5, of which 5 were waited for; matrix products, arithmetic and copies ran while one was open for 3% of the time, Pallas kernels for 0%

commit v1 on v0

--- a/solution.py
+++ b/solution.py
@@ -59,7 +59,9 @@
     )
     all_keys, all_values = (
         lax.all_gather(keys_normed, "blk", axis=0, tiled=True),
-        lax.all_gather(values_block, "blk", axis=0, tiled=True),
+        jnp.concatenate(
+            lax.all_to_all(jnp.stack([values_block] * lax.axis_size("blk")), "blk", 0, 0), axis=0
+        ),
     )
     group_count = lax.axis_size("blk")
     per_block = 1

time: 1440 us -> 1200 us (0.83)
  waiting for transfers between devices: 1350 us -> 1100 us
    all_gather x1 -> x0, waiting for transfers between devices: 311 us -> none  [body(): lax.all_gather(values_block, 'blk', axis=0, tiled=True)]
    all_gather x1, waiting for transfers between devices: 268 us -> 345 us  [body(): lax.all_gather(keys_normed, 'blk', axis=0, tiled=True)]
    all_gather x1, waiting for transfers between devices: 275 us -> 258 us  [body(): lax.all_gather(out_weights, 'blk', axis=2, tiled=True)]
    unnamed x6 -> x5, waiting for transfers between devices: 76.1 us -> 77.1 us
  transfers between devices with their start and end apart: 5 -> 5, of which waited for: 5 -> 4; matrix products, arithmetic and copies ran while one was open for 3% -> 3% of each run, Pallas kernels for 0% -> 0%
where the time goes in v1:
time: 1200 us
  waiting for transfers between devices  1100 us (92%)
  local copies, waits for them, and re-layouts  29.8 us (2%)
  matrix products  20.8 us (2%)
  between operations  13.3 us (1%)
  blocking collectives  12.7 us (1%)
    all_gather x1, waiting for transfers between devices, body(): lax.all_gather(qkv_weights, 'blk', axis=2, tiled=True)  424 us
    all_gather x1, waiting for transfers between devices, body(): lax.all_gather(keys_normed, 'blk', axis=0, tiled=True)  345 us
    all_gather x1, waiting for transfers between devices, body(): lax.all_gather(out_weights, 'blk', axis=2, tiled=True)  258 us
    unnamed x5, waiting for transfers between devices  77.1 us
  transfers between devices with their start and end apart: 5, of which 4 were waited for; matrix products, arithmetic and copies ran while one was open for 3% of the time, Pallas kernels for 0%

profile of v1, /device:TPU:1, one launch (start us, length us, event | category | flops | bytes accessed | tf_op | source)
XLA Modules:
  0.0 1196.7 jit_solution(16570385090877557660)
XLA Ops:
  6.5 0.7 all-gather.4.cloned.1.call-update
  7.3 1.1 fusion.17
  8.4 0.9 pad_maximum_fusion
  9.3 12.7 %all_gather.12 = bf16[2,96,2560]{2,1,0:T(8,128)(2,1)S(1)} all-gather(bf16[2,24,2560]{2,1,0:T(8,128)(2,1)S(1)} %pad_maximum_fusion), channel_id=1, replica_groups=mesh['blk'=64,'uly'=4] {'uly'}, dimensions={1}, use_global_device_ids=true | all-gather | bytes 1228800 | tf_op jit(solution)/shard_map/all_gather | solution.py:26
  22.0 423.9 %all-gather.4.cloned.1.call-done = bf16[2,3,2560,640]{3,2,1,0:T(8,128)(2,1)} async-done(((bf16[2,3,40,640]{3,2,1,0:T(8,128)(2,1)}), bf16[2,3,2560,640]{3,2,1,0:T(8,128)(2,1)}) %all-gather.4.cloned.1.call-update) | async-done | bytes 19660816 | tf_op jit(solution)/shard_map/all_gather | solution.py:31
  445.9 8.3 convolution_bitcast_fusion.1
  454.2 0.2 fusion.5
  454.4 0.2 copy.39
  454.8 0.7 fusion.8
  455.6 3.7 stack.21
  459.3 8.3 all-to-all-start
  467.6 0.7 all-gather.8.cloned.1.call-update
  468.4 0.2 copy.41
  468.9 344.9 %all-gather.6.cloned.1.call-done = bf16[6144,640]{1,0:T(8,128)(2,1)} async-done(((bf16[96,640]{1,0:T(8,128)(2,1)}), bf16[6144,640]{1,0:T(8,128)(2,1)}) %all-gather.6.cloned.1.call-update) | async-done | bytes 7864336 | tf_op jit(solution)/shard_map/all_gather | solution.py:61
  813.9 31.7 %while.13 = (s32[]{:T(128)}, f32[96,5,128]{2,0,1:T(8,128)S(1)}, f32[96,5]{0,1:T(8,128)S(1)}, bf16[8,768,640]{2,1,0:T(8,128)(2,1)}, bf16[8,768,640]{2,1,0:T(8,128...) while((s32[]{:T(128)}, f32[96,5,128]{2,0,1:T(8,128)S(1)}, ...), condition=%wide.region_4.5_spmd.clone, body=%wide.region_2.4_spmd.clone.sunk | while | flops 190341600 | bytes 11927140 | solution.py:78
  813.9 1.7 constant_dynamic-slice_fusion.3
  815.5 0.6 copy.62
  816.2 0.5 convert_reduce_fusion.2
  816.7 0.6 copy.61
  817.3 0.5 fusion.35
  817.8 1.7 constant_dynamic-slice_fusion.3
  819.5 0.6 copy.62
  820.2 0.5 convert_reduce_fusion.2
  820.6 0.6 copy.61
  821.3 0.5 fusion.35
  821.8 1.7 constant_dynamic-slice_fusion.3
  823.5 0.6 copy.62
  824.1 0.5 convert_reduce_fusion.2
  824.6 0.6 copy.61
  825.3 0.5 fusion.35
  825.8 1.7 constant_dynamic-slice_fusion.3
  827.4 0.6 copy.62
  828.1 0.5 convert_reduce_fusion.2
  828.6 0.6 copy.61
  829.2 0.5 fusion.35
  829.7 1.7 constant_dynamic-slice_fusion.3
  831.4 0.6 copy.62
  832.1 0.5 convert_reduce_fusion.2
  832.5 0.6 copy.61
  833.2 0.5 fusion.35
  833.7 1.7 constant_dynamic-slice_fusion.3
  835.4 0.6 copy.62
  836.0 0.5 convert_reduce_fusion.2
  836.5 0.6 copy.61
  837.2 0.5 fusion.35
  837.7 1.7 constant_dynamic-slice_fusion.3
  839.3 0.6 copy.62
  840.0 0.5 convert_reduce_fusion.2
  840.5 0.6 copy.61
  841.1 0.5 fusion.35
  841.6 1.7 constant_dynamic-slice_fusion.3
  843.3 0.6 copy.62
  844.0 0.5 convert_reduce_fusion.2
  844.5 0.6 copy.61
  845.1 0.5 fusion.35
  845.9 0.2 copy.45
  846.1 0.2 copy.47
  846.4 1.0 fusion.18
  847.4 258.4 %all-gather.8.cloned.1.call-done = bf16[2,640,2560]{1,2,0:T(8,128)(2,1)} async-done(((bf16[2,640,40]{1,2,0:T(8,128)(2,1)}), bf16[2,640,2560]{1,2,0:T(8,128)(2,1)}) %all-gather.8.cloned.1.call-update) | async-done | bytes 6553616 | tf_op jit(solution)/shard_map/all_gather | solution.py:86
  1105.8 5.0 fusion.1
  1110.8 1.0 copy.57
  1111.9 75.7 %reduce-scatter.4.cloned.1.call-done = bf16[24,5120]{1,0:T(8,128)(2,1)} async-done(((bf16[96,5120]{1,0:T(8,128)(2,1)}), bf16[24,5120]{1,0:T(8,128)(2,1)}) %reduce-scatter.4.cloned.1.call-update) | async-done | bytes 245776
  1187.6 1.0 bitcast_convert_fusion
  1188.5 1.7 fusion.11
  (36 shorter events, 1.3 us)
Async XLA Ops:
  6.5 439.4 %all-gather.4.cloned.1.call-start = ((), (), s32[]{:S(2)}) async-start(), calls=%async_computation.2 | async-start | bytes 19968000 | tf_op jit(solution)/shard_map/all_gather | solution.py:31
  7.3 806.6 %all-gather.6.cloned.1.call-start = ((), (), s32[]{:S(2)}) async-start(), calls=%async_computation.3 | async-start | bytes 7987200 | tf_op jit(solution)/shard_map/all_gather | solution.py:61
  22.0 432.2 %copy-start = (s32[96,3,640]{2,0,1:T(8,128)S(1)}, s32[96,3,640]{2,0,1:T(8,128)}, u32[]{:S(2)}) copy-start(s32[96,3,640]{2,0,1:T(8,128)} %param.14) | copy-start | bytes 2211844
  22.0 432.8 %copy-start.1 = (f32[640]{0:T(1024)S(1)}, f32[640]{0:T(1024)}, u32[]{:S(2)}) copy-start(f32[640]{0:T(1024)} %param.16) | copy-start | bytes 7684
  459.3 9.3 copy-start.2
  459.3 354.6 %all-to-all-start = ((bf16[64,96,640]{2,1,0:T(8,128)(2,1)}), bf16[64,96,640]{2,1,0:T(8,128)(2,1)}, u32[]{:S(2)}, u32[]{:S(2)}) async-start(bf16[64,96,640]{2,1,0:T(8,128)(2,1)} %stack.21), calls=%async_computation | async-start | bytes 15728640 | tf_op jit(solution)/shard_map/all_to_all | solution.py:63
  467.6 638.3 %all-gather.8.cloned.1.call-start = ((), (), s32[]{:S(2)}) async-start(), calls=%async_computation.4 | async-start | bytes 6656000 | tf_op jit(solution)/shard_map/all_gather | solution.py:86
  468.3 719.3 %reduce-scatter.4.cloned.1.call-start = ((), (), s32[]{:S(2)}) async-start(), calls=%async_computation.5 | async-start | bytes 1228800
Sparse Core Ops, SparseCore 0:
  9.2 436.6 all-gather.3
  455.7 358.1 all-gather.5
  815.7 290.1 all-gather.7
  1112.0 75.5 reduce-scatter.3
